TPU v7x, 32 devices: a whole 2x2x4 slice. The times are simulated.
32 devices in a mesh: dp: 16 (over z, y, x), fsdp: 2 (over core).
Axes of the slice: x: 2, y: 2, z: 4, core: 2. Of those that a mesh axis runs over, the one named last changes fastest.
Arguments:
- tokens: bfloat16 [64, 512, 768], P(('dp', 'fsdp')), may hold values from -6 to 6
- cotangent: bfloat16 [64, 80, 768], P(('dp', 'fsdp')), may hold values from -6 to 6
- positions: int32 [64, 80], P(('dp', 'fsdp')), may hold values from 0 to 511, as said below
- counts: int32 [64], P(('dp', 'fsdp')), may hold values from 40 to 80
- query_key_value_weight: bfloat16 [2, 768, 2304], P(None, ('dp', 'fsdp')), may hold values from -0.21875 to 0.21875
- attention_output_weight: bfloat16 [2, 768, 768], P(None, ('dp', 'fsdp')), may hold values from -0.625 to 0.625
- feedforward_input_weight: bfloat16 [2, 768, 3072], P(None, ('dp', 'fsdp')), may hold values from -0.21875 to 0.21875
- feedforward_input_bias: bfloat16 [2, 3072], P(None, ('dp', 'fsdp')), may hold values from -3 to 3
- feedforward_output_weight: bfloat16 [2, 3072, 768], P(None, ('dp', 'fsdp')), may hold values from -0.109375 to 0.109375
- small: bfloat16 [2, 768, 24], P(None, ('dp', 'fsdp'))
- query_up_weight: float32 [2, 8, 768], replicated, may hold values from -1.2 to 1.2
- value_up_weight: float32 [2, 8, 768], replicated, may hold values from -1.2 to 1.2
Outputs:
- activations: bfloat16 [64, 512, 768], P(('dp', 'fsdp'))
- d_tokens: float32 [64, 512, 768], P(('dp', 'fsdp'))
- query_up_gradient: float32 [2, 8, 768], replicated
- value_up_gradient: float32 [2, 8, 768], replicated
Inputs may be any that keep to these rules, and one draw needn't show every extreme that they name: In each sequence the 80 entries are distinct positions; entry m is used where m < counts of that sequence.
All inputs are finite; a program needn't handle non-finite values.
Results may differ from a plain program's by a relative error of at most 0.03.
Values may be sent and summed in bfloat16 or wider, within the bound.
No kernel may reach another device: no remote copies, remote signals or barrier semaphores. Data moves between devices by JAX's collectives and lax.ppermute only.
A program may use at most 256 MiB of HBM per device.

v0:
```python
import jax
import jax.numpy as jnp
from jax import lax
from jax.sharding import PartitionSpec as P

MODEL_WIDTH = 768
H = 12
HD = 64
ADAPTER_RANK = 8
ENCODER_LAYERS = 2
LEN = 512
MAXM = 80
EPSILON = 1e-05


def layer_norm(value, norm_gain, norm_shift):
    average = jnp.mean(value, axis=-1, keepdims=True)
    centred = value - average
    spread = jnp.mean(centred * centred, axis=-1, keepdims=True)
    return centred * lax.rsqrt(spread + EPSILON) * norm_gain + norm_shift


def gelu_exact(value):
    return jax.nn.gelu(value, approximate=False)


def matrix_multiply(left, right):
    return jnp.dot(left, right, preferred_element_type=jnp.float32)


def transposed_multiply(left, right):
    return lax.dot_general(
        left, right, (((1,), (1,)), ((), ())), preferred_element_type=jnp.float32
    )


def leading_axis_contract(left, right):
    return lax.dot_general(
        left, right, (((0,), (0,)), ((), ())), preferred_element_type=jnp.float32
    )


def fetch_forward(layer_qkv, layer_o, layer_in, layer_bias, layer_out, layer_small):
    return (
        lax.all_gather(layer_qkv, ("dp", "fsdp"), axis=0, tiled=True),
        lax.all_gather(layer_o, ("dp", "fsdp"), axis=0, tiled=True),
        lax.all_gather(layer_in, ("dp", "fsdp"), axis=0, tiled=True),
        lax.all_gather(layer_bias, ("dp", "fsdp"), axis=0, tiled=True),
        lax.all_gather(layer_out, ("dp", "fsdp"), axis=0, tiled=True),
        lax.all_gather(layer_small, ("dp", "fsdp"), axis=0, tiled=True),
    )


def fetch_backward(layer_qkv, layer_o, layer_in, layer_bias, layer_out, layer_small):
    return (
        lax.all_gather(layer_qkv, ("dp", "fsdp"), axis=0, tiled=True),
        lax.all_gather(layer_o, ("dp", "fsdp"), axis=0, tiled=True),
        lax.all_gather(layer_in, ("dp", "fsdp"), axis=0, tiled=True),
        lax.all_gather(layer_bias, ("dp", "fsdp"), axis=0, tiled=True),
        lax.all_gather(layer_out, ("dp", "fsdp"), axis=0, tiled=True),
        lax.all_gather(layer_small, ("dp", "fsdp"), axis=0, tiled=True),
    )


def attend(packed_projection):
    heads_view = packed_projection.reshape(LEN, 3, H, HD)
    query_rows = heads_view[:, 0]
    key_rows = heads_view[:, 1]
    value_matrix_rows = heads_view[:, 2]
    scores = (
        jnp.einsum("qhd,khd->hqk", query_rows, key_rows, preferred_element_type=jnp.float32) * 0.125
    )
    row_max = jnp.max(scores, axis=-1, keepdims=True)
    powers = jnp.exp(scores - row_max)
    row_sum = jnp.sum(powers, axis=-1, keepdims=True)
    soft_probs = (powers / row_sum).astype(jnp.bfloat16)
    context = jnp.einsum(
        "hqk,khd->qhd", soft_probs, value_matrix_rows, preferred_element_type=jnp.float32
    )
    return (
        context.reshape(LEN, H * HD).astype(jnp.bfloat16),
        (row_max + jnp.log(row_sum))[:, :, 0],
    )


def attend_back(element):
    packed_projection, logsumexp_total, d_context = element
    heads_view = packed_projection.reshape(LEN, 3, H, HD)
    query_rows = heads_view[:, 0]
    key_rows = heads_view[:, 1]
    value_matrix_rows = heads_view[:, 2]
    grad_view = d_context.reshape(LEN, H, HD)
    scores = (
        jnp.einsum("qhd,khd->hqk", query_rows, key_rows, preferred_element_type=jnp.float32) * 0.125
    )
    soft_probs = jnp.exp(scores - logsumexp_total[:, :, None])
    d_probs = jnp.einsum(
        "qhd,khd->hqk", grad_view, value_matrix_rows, preferred_element_type=jnp.float32
    )
    d_scores = (
        soft_probs * (d_probs - jnp.sum(soft_probs * d_probs, axis=-1, keepdims=True))
    ).astype(jnp.bfloat16)
    d_queries = (
        jnp.einsum("hqk,khd->qhd", d_scores, key_rows, preferred_element_type=jnp.float32) * 0.125
    ).astype(jnp.bfloat16)
    d_keys = (
        jnp.einsum("hqk,qhd->khd", d_scores, query_rows, preferred_element_type=jnp.float32) * 0.125
    ).astype(jnp.bfloat16)
    d_values = jnp.einsum(
        "hqk,qhd->khd",
        soft_probs.astype(jnp.bfloat16),
        grad_view,
        preferred_element_type=jnp.float32,
    ).astype(jnp.bfloat16)
    return jnp.stack([d_queries, d_keys, d_values], axis=1).reshape(LEN, 3 * H * HD)


def layer_forward_pass(hidden_state, collected_rows, query_adapter_output, value_adapter_output):
    (
        query_key_value_weight,
        attention_output_weight,
        feedforward_input_weight,
        feedforward_input_bias,
        feedforward_output_weight,
        small,
    ) = collected_rows
    params = small.astype(jnp.float32)
    rounded_input = hidden_state.astype(jnp.bfloat16)
    adapter_down_weight = matrix_multiply(rounded_input, small[:, 8 : 8 + 2 * ADAPTER_RANK]).astype(
        jnp.bfloat16
    )
    adapter_up_weight = jnp.concatenate(
        [
            2.0
            * matrix_multiply(
                adapter_down_weight[:, :ADAPTER_RANK], query_adapter_output.astype(jnp.bfloat16)
            ),
            jnp.zeros_like(hidden_state),
            2.0
            * matrix_multiply(
                adapter_down_weight[:, ADAPTER_RANK:], value_adapter_output.astype(jnp.bfloat16)
            ),
        ],
        axis=1,
    )
    bias_vector_row = jnp.concatenate([params[:, 0], jnp.zeros_like(params[:, 0]), params[:, 1]])
    packed_projection = (
        matrix_multiply(rounded_input, query_key_value_weight) + bias_vector_row + adapter_up_weight
    ).astype(jnp.bfloat16)
    context, logsumexp_total = lax.map(attend, packed_projection.reshape(-1, LEN, 3 * MODEL_WIDTH))
    context = context.reshape(-1, MODEL_WIDTH)
    leading_partial_sum = hidden_state + (
        matrix_multiply(context, attention_output_weight) + params[:, 2]
    )
    normed = layer_norm(leading_partial_sum, params[:, 3], params[:, 4])
    preactivation_input = matrix_multiply(
        normed.astype(jnp.bfloat16), feedforward_input_weight
    ) + feedforward_input_bias.astype(jnp.float32)
    trailing_partial_sum = normed + (
        matrix_multiply(
            gelu_exact(preactivation_input).astype(jnp.bfloat16), feedforward_output_weight
        )
        + params[:, 5]
    )
    layer_output = layer_norm(trailing_partial_sum, params[:, 6], params[:, 7])
    return (
        layer_output,
        (
            packed_projection,
            adapter_down_weight,
            logsumexp_total,
            leading_partial_sum,
            preactivation_input,
            trailing_partial_sum,
        ),
    )


def layer_backward_pass(
    incoming_gradient, saved_state, collected_rows, query_adapter_output, value_adapter_output
):
    (
        query_key_value_weight,
        attention_output_weight,
        feedforward_input_weight,
        feedforward_input_bias,
        feedforward_output_weight,
        small,
    ) = collected_rows
    params = small.astype(jnp.float32)
    (
        packed_projection,
        adapter_down_weight,
        logsumexp_total,
        leading_partial_sum,
        preactivation_input,
        trailing_partial_sum,
    ) = saved_state
    unused_second, second_back = jax.vjp(
        lambda value: layer_norm(value, params[:, 6], params[:, 7]), trailing_partial_sum
    )
    d_second = second_back(incoming_gradient)[0]
    d_act = transposed_multiply(d_second.astype(jnp.bfloat16), feedforward_output_weight)
    unused_gelu, gelu_back = jax.vjp(gelu_exact, preactivation_input)
    d_pre = gelu_back(d_act)[0].astype(jnp.bfloat16)
    d_normed = d_second + transposed_multiply(d_pre, feedforward_input_weight)
    unused_first, first_back = jax.vjp(
        lambda value: layer_norm(value, params[:, 3], params[:, 4]), leading_partial_sum
    )
    d_first = first_back(d_normed)[0]
    d_context = transposed_multiply(d_first.astype(jnp.bfloat16), attention_output_weight).astype(
        jnp.bfloat16
    )
    d_packed = lax.map(
        attend_back,
        (
            packed_projection.reshape(-1, LEN, 3 * MODEL_WIDTH),
            logsumexp_total,
            d_context.reshape(-1, LEN, MODEL_WIDTH),
        ),
    )
    d_packed = d_packed.reshape(-1, 3 * MODEL_WIDTH)
    query_adapter_gradient = d_packed[:, :MODEL_WIDTH]
    value_adapter_gradient = d_packed[:, 2 * MODEL_WIDTH :]
    d_down = jnp.concatenate(
        [
            2.0
            * transposed_multiply(
                query_adapter_gradient, query_adapter_output.astype(jnp.bfloat16)
            ),
            2.0
            * transposed_multiply(
                value_adapter_gradient, value_adapter_output.astype(jnp.bfloat16)
            ),
        ],
        axis=1,
    ).astype(jnp.bfloat16)
    query_gradient_total = 2.0 * leading_axis_contract(
        adapter_down_weight[:, :ADAPTER_RANK], query_adapter_gradient
    )
    value_gradient_total = 2.0 * leading_axis_contract(
        adapter_down_weight[:, ADAPTER_RANK:], value_adapter_gradient
    )
    d_input = (
        d_first
        + transposed_multiply(d_packed, query_key_value_weight)
        + transposed_multiply(d_down, small[:, 8 : 8 + 2 * ADAPTER_RANK])
    )
    return (d_input, query_gradient_total, value_gradient_total)


def on_device(
    tokens,
    cotangent,
    positions,
    counts,
    query_key_value_weight,
    attention_output_weight,
    feedforward_input_weight,
    feedforward_input_bias,
    feedforward_output_weight,
    small,
    query_up_weight,
    value_up_weight,
):
    hidden_state = tokens.reshape(-1, MODEL_WIDTH).astype(jnp.float32)
    saved_state_stack = []
    gathered_all = []
    for layer_index in range(ENCODER_LAYERS):
        collected_rows = fetch_forward(
            query_key_value_weight[layer_index],
            attention_output_weight[layer_index],
            feedforward_input_weight[layer_index],
            feedforward_input_bias[layer_index],
            feedforward_output_weight[layer_index],
            small[layer_index],
        )
        hidden_state, saved_state = layer_forward_pass(
            hidden_state, collected_rows, query_up_weight[layer_index], value_up_weight[layer_index]
        )
        saved_state_stack.append(saved_state)
        gathered_all.append(collected_rows)
    activations = hidden_state.astype(jnp.bfloat16).reshape(tokens.shape)
    is_live = jnp.arange(MAXM)[None, :] < counts[:, None]
    indicator_matrix = (
        (positions[:, :, None] == jnp.arange(LEN)[None, None, :]) & is_live[:, :, None]
    ).astype(jnp.bfloat16)
    incoming_gradient = jnp.einsum(
        "nkw,nkq->nwq", indicator_matrix, cotangent, preferred_element_type=jnp.float32
    ).reshape(-1, MODEL_WIDTH)
    query_gradient_stack = [None] * ENCODER_LAYERS
    value_gradient_stack = [None] * ENCODER_LAYERS
    for layer_index in reversed(range(ENCODER_LAYERS)):
        collected_rows = fetch_backward(
            query_key_value_weight[layer_index],
            attention_output_weight[layer_index],
            feedforward_input_weight[layer_index],
            feedforward_input_bias[layer_index],
            feedforward_output_weight[layer_index],
            small[layer_index],
        )
        incoming_gradient, query_gradient_total, value_gradient_total = layer_backward_pass(
            incoming_gradient,
            saved_state_stack[layer_index],
            collected_rows,
            query_up_weight[layer_index],
            value_up_weight[layer_index],
        )
        query_gradient_total, value_gradient_total = lax.psum(
            (query_gradient_total, value_gradient_total), ("dp", "fsdp")
        )
        query_gradient_stack[layer_index] = query_gradient_total
        value_gradient_stack[layer_index] = value_gradient_total
    query_up_gradient = jnp.stack(query_gradient_stack)
    value_up_gradient = jnp.stack(value_gradient_stack)
    return (
        activations,
        incoming_gradient.reshape(tokens.shape),
        query_up_gradient,
        value_up_gradient,
    )


def solution(mesh):
    in_specs = (
        P(("dp", "fsdp"), None, None),
        P(("dp", "fsdp"), None, None),
        P(("dp", "fsdp"), None),
        P(("dp", "fsdp")),
        P(None, ("dp", "fsdp"), None),
        P(None, ("dp", "fsdp"), None),
        P(None, ("dp", "fsdp"), None),
        P(None, ("dp", "fsdp")),
        P(None, ("dp", "fsdp"), None),
        P(None, ("dp", "fsdp"), None),
        P(),
        P(),
    )
    out_specs = (P(("dp", "fsdp"), None, None), P(("dp", "fsdp"), None, None), P(), P())
    return jax.shard_map(
        on_device, mesh=mesh, in_specs=in_specs, out_specs=out_specs, check_vma=False
    )
```

profile of v0, /device:TPU:8, one launch (start us, length us, event | category | flops | bytes accessed | tf_op | source)
XLA Modules:
  0.0 912.4 jit_solution(5408790582590353400)
XLA Ops:
  17.6 36.0 %all-gather.7 = bf16[1,768,24]{2,1,0:T(8,128)(2,1)S(1)} all-gather(bf16[1,24,24]{2,1,0:T(8,128)(2,1)S(1)} %get-tuple-element.249), channel_id=9, replica_groups=mesh['dp'=16,'fsdp'=2] {'dp','fsdp'}, dimensions={1}, use_global_device_ids=true | all-gather | bytes 38016 | tf_op jit(solution)/shard_map/all_gather | solution.py:50
  56.3 37.5 %all-gather.1 = bf16[1,768,24]{2,1,0:T(8,128)(2,1)S(1)} all-gather(bf16[1,24,24]{2,1,0:T(8,128)(2,1)S(1)} %get-tuple-element.250), channel_id=3, replica_groups=mesh['dp'=16,'fsdp'=2] {'dp','fsdp'}, dimensions={1}, use_global_device_ids=true | all-gather | bytes 38016 | tf_op jit(solution)/shard_map/all_gather | solution.py:50
  99.7 45.6 %all-reduce.3 = (bf16[3072]{0:T(1024)(128)(2,1)S(1)}, bf16[3072]{0:T(1024)(128)(2,1)S(1)}) all-reduce(bf16[3072]{0:T(1024)(128)(2,1)S(1)} %dynamic-update-slice, bf16[3072]{0:T(1024)(128)(2,1)S(1)} %dynamic-update-slice.1), channel_id=6, replica_groups=mesh['dp'=16,'fsdp'=2] {'dp','fsdp'}, use_global_device_ids=true, to_apply=%add | all-reduce | flops 6144 | bytes 24576
  149.0 9.4 %fusion.54 = bf16[1024,2304]{1,0:T(8,128)(2,1)} fusion(f32[1024,768]{1,0:T(8,128)S(1)} %convolution_multiply_fusion.2, f32[1024,768]{1,0:T(8,128)} %convolution_multiply_fusion.3, bf16[1024,768]{1,0:T(8,128)(2,1)} %bitcast.377, f32[2304]{0:T(1024)S(1)} %get-tuple-element.255, f32[2304]{0:T(1024)S(1)} %get-tuple-element.254, ...), kind=kOutput, calls=%fused_computation.111 | convolution fusion | flops 3635675136 | bytes 16140288 | tf_op jit(solution)/shard_map/dot_general | solution.py:28
  158.4 6.6 copy.66
  165.1 18.2 %while.44 = (s32[]{:T(128)}, bf16[2,512,768]{2,1,0:T(8,128)(2,1)S(1)}, f32[2,12,512]{2,1,0:T(8,128)S(1)}, bf16[2,512,2304]{1,2,0:T(8,128)(2,1)}, s32[]{:T(128)}) while((s32[]{:T(128)}, bf16[2,512,768]{2,1,0:T(8,128)(2,1)S(1)}, f32[2,12,512]{2,1,0:T(8,128)S(1)}, bf16[2,512,2304]{1,2,0:T(8,128)(2,1)}, s32[]{:T(128)}) %tuple.124), condition=%wide.region_3.4_spmd, body=%wide.region_0.3_spmd.sunk | while | flops 834004992 | bytes 48996424 | solution.py:150
  171.0 2.8 fusion.283
  180.0 2.8 fusion.283
  184.5 3.8 fusion.235
  188.9 6.6 all-gather.25.cloned.1.call-done
  195.5 36.3 %fusion.42 = (f32[1024,3072]{1,0:T(8,128)}, f32[1024,3072]{1,0:T(8,128)}) fusion(f32[3072]{0:T(1024)S(1)} %convert_element_type.210, bf16[1,768,3072]{2,1,0:T(8,128)(2,1)} %all-gather.25.cloned.1.call-done, f32[1024,768]{1,0:T(8,128)S(1)} %get-tuple-element.259, f32[768]{0:T(1024)S(1)} %get-tuple-element.177, f32[768]{0:T(1024)S(1)} %get-tuple-element.178, ...), kind=kOutput, calls=%fused_computation.78 | convolution fusion | flops 5033951232 | bytes 33056768 | tf_op jit(solution)/shard_map/dot_general | solution.py:28
  231.8 29.0 %all-gather.27.cloned.1.call-done = bf16[1,3072,768]{2,1,0:T(8,128)(2,1)} async-done(((bf16[1,96,768]{2,1,0:T(8,128)(2,1)}), bf16[1,3072,768]{2,1,0:T(8,128)(2,1)}) %all-gather.27.cloned.1.call-update) | async-done | bytes 4718608 | tf_op jit(solution)/shard_map/all_gather | solution.py:49
  260.8 12.7 %fusion.236 = (f32[1024]{0:T(1024)S(1)}, f32[1024,768]{1,0:T(8,128)S(1)}) fusion(f32[768]{0:T(1024)S(1)} %copy-done.73, bf16[1,3072,768]{2,1,0:T(8,128)(2,1)} %all-gather.27.cloned.1.call-done, f32[1024,3072]{1,0:T(8,128)} %get-tuple-element.260, f32[1024,3072]{1,0:T(8,128)} %get-tuple-element.261, f32[3072]{0:T(1024)S(1)} %convert_element_type.210, ...), kind=kOutput, calls=%fused_computation.320 | convolution fusion | flops 4849925120 | bytes 36209664 | tf_op jit(solution)/shard_map/dot_general | solution.py:28
  279.9 41.6 %all-gather.29.cloned.1.call-done = bf16[1,768,2304]{2,1,0:T(8,128)(2,1)} async-done(((bf16[1,24,2304]{2,1,0:T(8,128)(2,1)}), bf16[1,768,2304]{2,1,0:T(8,128)(2,1)}) %all-gather.29.cloned.1.call-update) | async-done | bytes 3538960 | tf_op jit(solution)/shard_map/all_gather | solution.py:45
  321.4 8.5 fusion.55
  330.0 6.7 copy.70
  336.8 18.5 %while.45 = (s32[]{:T(128)}, bf16[2,512,768]{2,1,0:T(8,128)(2,1)S(1)}, f32[2,12,512]{2,1,0:T(8,128)S(1)}, bf16[2,512,2304]{1,2,0:T(8,128)(2,1)}, s32[]{:T(128)}) while((s32[]{:T(128)}, bf16[2,512,768]{2,1,0:T(8,128)(2,1)S(1)}, f32[2,12,512]{2,1,0:T(8,128)S(1)}, bf16[2,512,2304]{1,2,0:T(8,128)(2,1)}, s32[]{:T(128)}) %tuple.127), condition=%wide.region_11.12_spmd, body=%wide.region_8.11_spmd.sunk | while | flops 834004992 | bytes 48996424 | solution.py:150
  343.1 2.8 fusion.285
  352.1 2.8 fusion.285
  355.3 22.0 %all-gather.31.cloned.1.call-done = bf16[1,768,768]{2,1,0:T(8,128)(2,1)} async-done(((bf16[1,24,768]{2,1,0:T(8,128)(2,1)}), bf16[1,768,768]{2,1,0:T(8,128)(2,1)}) %all-gather.31.cloned.1.call-update) | async-done | bytes 1179664 | tf_op jit(solution)/shard_map/all_gather | solution.py:46
  377.3 4.5 fusion.237
  382.3 61.8 %all-gather.33.cloned.1.call-done = bf16[1,768,3072]{2,1,0:T(8,128)(2,1)} async-done(((bf16[1,24,3072]{2,1,0:T(8,128)(2,1)}), bf16[1,768,3072]{2,1,0:T(8,128)(2,1)}) %all-gather.33.cloned.1.call-update) | async-done | bytes 4718608 | tf_op jit(solution)/shard_map/all_gather | solution.py:47
  444.1 36.5 %fusion.43 = (f32[1024,3072]{1,0:T(8,128)}, f32[1024,3072]{1,0:T(8,128)}) fusion(f32[3072]{0:T(1024)S(1)} %copy-done.66, bf16[1,768,3072]{2,1,0:T(8,128)(2,1)} %all-gather.33.cloned.1.call-done, f32[1024,768]{1,0:T(8,128)S(1)} %get-tuple-element.265, f32[768]{0:T(1024)S(1)} %copy-done.71, f32[768]{0:T(1024)S(1)} %copy-done.69, f32[1024]{0:T(1024)S(1)} %fusion.214, ...), kind=kOutput, calls=%fused_computation.79 | convolution fusion | flops 5033951232 | bytes 33056768 | tf_op jit(solution)/shard_map/dot_general | solution.py:28
  480.6 28.8 %all-gather.35.cloned.1.call-done = bf16[1,3072,768]{2,1,0:T(8,128)(2,1)} async-done(((bf16[1,96,768]{2,1,0:T(8,128)(2,1)}), bf16[1,3072,768]{2,1,0:T(8,128)(2,1)}) %all-gather.35.cloned.1.call-update) | async-done | bytes 4718608 | tf_op jit(solution)/shard_map/all_gather | solution.py:49
  509.5 12.6 %fusion.238 = (f32[1024]{0:T(1024)S(1)}, f32[1024,768]{1,0:T(8,128)S(1)}) fusion(f32[768]{0:T(1024)S(1)} %copy-done.70, bf16[1,3072,768]{2,1,0:T(8,128)(2,1)} %all-gather.35.cloned.1.call-done, f32[1024,3072]{1,0:T(8,128)} %get-tuple-element.266, f32[1024,3072]{1,0:T(8,128)} %get-tuple-element.267, f32[3072]{0:T(1024)S(1)} %copy-done.66, ...), kind=kOutput, calls=%fused_computation.322 | convolution fusion | flops 4849925120 | bytes 36209664 | tf_op jit(solution)/shard_map/dot_general | solution.py:28
  523.0 3.4 fusion.229
  526.4 22.2 %multiply_reduce_fusion.6 = (f32[1024]{0:T(1024)S(1)}, f32[1024,768]{1,0:T(8,128)}) fusion(f32[1024,768]{1,0:T(8,128)S(1)} %get-tuple-element.265, f32[1024]{0:T(1024)S(1)} %broadcast_multiply_fusion.1, f32[768]{0:T(1024)S(1)} %copy-done.69, bf16[1,768,3072]{2,1,0:T(8,128)(2,1)} %all-gather.33.cloned.1.call-done, f32[1024,3072]{1,0:T(8,128)} %get-tuple-element.266, ...), kind=kOutput, calls=%fused_computation.150 | convolution fusion | flops 9717152768 | bytes 44067840 | tf_op jit(solution)/shard_map/dot_general | solution.py:32
  548.7 2.8 fusion.228
  553.1 2.6 convolution_convert_fusion.1
  555.7 2.5 broadcast.342.clone2
  558.2 83.9 %while.46 = (s32[]{:T(128)}, bf16[2,512,2304]{2,1,0:T(8,128)(2,1)}, bf16[2,512,2304]{1,2,0:T(8,128)(2,1)}, f32[2,12,512]{2,1,0:T(8,128)S(1)}, bf16[2,512,768]{2,1,0:T(8,128)(2,1)}, /*index=5*/s32[]{:T(128)}) while((s32[]{:T(128)}, bf16[2,512,2304]{2,1,0:T(8,128)(2,1)}, bf16[2,512,2304]{1,2,0:T(8,128)(2,1)}, f32[2,12,512]{2,1,0:T(8,128)S(1)}, ...), condition=%wide.region_22.23_spmd, body=%wide.region_20.22_spmd.sunk | while | flops 2055333888 | bytes 168870656 | solution.py:214
  560.3 6.4 fusion.291
  569.9 11.5 %multiply_reduce_fusion.18 = (f32[12,512]{1,0:T(8,128)S(1)}, f32[12,512,512]{1,2,0:T(8,128)}) fusion(f32[12,512,512]{1,2,0:T(8,128)} %fusion.291, f32[12,512]{1,0:T(8,128)S(1)} %dynamic-slice_bitcast_fusion.4, bf16[512,12,64]{0,2,1:T(8,128)(2,1)S(1)} %bitcast.347, bf16[512,3,12,64]{0,3,2,1:T(8,128)(2,1)S(1)} %bitcast.338), kind=kOutput, calls=%fused_computation.29.clone.1 | convolution fusion | flops 415229952 | bytes 26796032 | tf_op jit(solution)/shard_map/while/body/eval_jaxpr/qhd,khd->hqk/dot_general | solution.py:97
  581.5 6.9 multiply_convert_fusion.16
  591.5 2.4 fusion.292
  594.2 2.6 copy.109
  596.8 3.2 constant_dynamic-update-slice_fusion.10
  601.9 6.4 fusion.291
  611.5 11.5 %multiply_reduce_fusion.18 = (f32[12,512]{1,0:T(8,128)S(1)}, f32[12,512,512]{1,2,0:T(8,128)}) fusion(f32[12,512,512]{1,2,0:T(8,128)} %fusion.291, f32[12,512]{1,0:T(8,128)S(1)} %dynamic-slice_bitcast_fusion.4, bf16[512,12,64]{0,2,1:T(8,128)(2,1)S(1)} %bitcast.347, bf16[512,3,12,64]{0,3,2,1:T(8,128)(2,1)S(1)} %bitcast.338), kind=kOutput, calls=%fused_computation.29.clone.1 | convolution fusion | flops 415229952 | bytes 26796032 | tf_op jit(solution)/shard_map/while/body/eval_jaxpr/qhd,khd->hqk/dot_general | solution.py:97
  623.1 6.9 multiply_convert_fusion.16
  633.1 2.4 fusion.292
  635.8 2.6 copy.109
  638.4 3.3 constant_dynamic-update-slice_fusion.10
  642.1 2.5 fusion.174
  649.4 6.0 fusion.84
  659.8 21.1 %multiply_reduce_fusion.4 = (f32[1024]{0:T(1024)S(1)}, f32[1024,768]{1,0:T(8,128)}) fusion(f32[1024,768]{1,0:T(8,128)S(1)} %copy-done.7, f32[1024]{0:T(1024)S(1)} %copy-done.46, f32[768]{0:T(1024)S(1)} %copy-done.68, bf16[1,768,3072]{2,1,0:T(8,128)(2,1)} %all-gather.25.cloned.1.call-done, f32[1024,3072]{1,0:T(8,128)} %get-tuple-element.260, ...), kind=kOutput, calls=%fused_computation.146 | convolution fusion | flops 9717152768 | bytes 44067840 | tf_op jit(solution)/shard_map/dot_general | solution.py:32
  681.0 2.8 fusion.226
  685.4 2.6 convolution_convert_fusion
  688.0 2.5 broadcast.342.clone
  690.6 82.5 %while.47 = (s32[]{:T(128)}, bf16[2,512,2304]{2,1,0:T(8,128)(2,1)}, bf16[2,512,2304]{1,2,0:T(8,128)(2,1)}, f32[2,12,512]{2,1,0:T(8,128)S(1)}, bf16[2,512,768]{2,1,0:T(8,128)(2,1)}, /*index=5*/s32[]{:T(128)}) while((s32[]{:T(128)}, bf16[2,512,2304]{2,1,0:T(8,128)(2,1)}, bf16[2,512,2304]{1,2,0:T(8,128)(2,1)}, f32[2,12,512]{2,1,0:T(8,128)S(1)}, ...), condition=%wide.region_29.30_spmd, body=%wide.region_27.29_spmd.sunk | while | flops 2055333888 | bytes 168477376 | solution.py:214
  692.6 6.3 fusion.300
  701.4 11.5 %multiply_reduce_fusion.19 = (f32[12,512]{1,0:T(8,128)S(1)}, f32[12,512,512]{1,2,0:T(8,128)}) fusion(f32[12,512,512]{1,2,0:T(8,128)} %fusion.300, f32[12,512]{1,0:T(8,128)S(1)} %dynamic-slice_bitcast_fusion.5, bf16[512,12,64]{0,2,1:T(8,128)(2,1)S(1)} %bitcast.349, bf16[512,3,12,64]{0,3,2,1:T(8,128)(2,1)S(1)} %bitcast.342), kind=kOutput, calls=%fused_computation.53.clone.1 | convolution fusion | flops 415229952 | bytes 26796032 | tf_op jit(solution)/shard_map/while/body/eval_jaxpr/qhd,khd->hqk/dot_general | solution.py:97
  713.4 6.9 multiply_convert_fusion.17
  723.4 2.4 fusion.301
  726.1 2.5 copy.111
  728.6 3.3 constant_dynamic-update-slice_fusion.11
  733.7 6.3 fusion.300
  742.5 11.5 %multiply_reduce_fusion.19 = (f32[12,512]{1,0:T(8,128)S(1)}, f32[12,512,512]{1,2,0:T(8,128)}) fusion(f32[12,512,512]{1,2,0:T(8,128)} %fusion.300, f32[12,512]{1,0:T(8,128)S(1)} %dynamic-slice_bitcast_fusion.5, bf16[512,12,64]{0,2,1:T(8,128)(2,1)S(1)} %bitcast.349, bf16[512,3,12,64]{0,3,2,1:T(8,128)(2,1)S(1)} %bitcast.342), kind=kOutput, calls=%fused_computation.53.clone.1 | convolution fusion | flops 415229952 | bytes 26796032 | tf_op jit(solution)/shard_map/while/body/eval_jaxpr/qhd,khd->hqk/dot_general | solution.py:97
  754.6 6.9 multiply_convert_fusion.17
  767.3 2.5 copy.111
  769.8 3.3 constant_dynamic-update-slice_fusion.11
  781.7 6.9 fusion.87
  788.7 2.6 add_add_fusion.4
  791.3 112.9 %all-reduce.6.cloned.1.call-done = (f32[1,8,768]{2,1,0:T(8,128)}, f32[1,8,768]{2,1,0:T(8,128)}, f32[1,8,768]{2,1,0:T(8,128)}, f32[1,8,768]{2,1,0:T(8,128)}) async-done(((f32[1,8,768]{2,1,0:T(8,128)}, f32[1,8,768]{2,1,0:T(8,128)}, f32[1,8,768]{2,1,0:T(8,128)}, f32[1,8,768]{2,1,0:T(8,128)}), (f32[1,8,768]{2,1,0:T(8,128)}, f32[1,8,768]{2,1,0:T(8,128)}, f32[1,8,768]{2,1,0:T(8,128)}, ...) | async-done | bytes 98320 | tf_op jit(solution)/shard_map/psum | solution.py:309
  (329 shorter events, 114.5 us)
Async XLA Ops:
  7.2 138.8 %copy-start = (bf16[2,80,768]{2,1,0:T(8,128)(2,1)S(1)}, bf16[2,80,768]{2,1,0:T(8,128)(2,1)}, u32[]{:S(2)}) copy-start(bf16[2,80,768]{2,1,0:T(8,128)(2,1)} %param.21) | copy-start | bytes 737284
  7.2 141.8 %all-gather.21.cloned.1.call-start = ((), (), s32[]{:S(2)}) async-start(), calls=%async_computation | async-start | bytes 3649536 | tf_op jit(solution)/shard_map/all_gather | solution.py:45
  9.0 174.5 %all-gather.23.cloned.1.call-start = ((), (), s32[]{:S(2)}) async-start(), calls=%async_computation.1 | async-start | bytes 1216512 | tf_op jit(solution)/shard_map/all_gather | solution.py:46
  10.5 185.0 %all-gather.25.cloned.1.call-start = ((), (), s32[]{:S(2)}) async-start(), calls=%async_computation.2 | async-start | bytes 4866048 | tf_op jit(solution)/shard_map/all_gather | solution.py:47
  12.3 83.3 %copy-start.40 = (f32[2,8,768]{2,1,0:T(8,128)S(1)}, f32[2,8,768]{2,1,0:T(8,128)}, u32[]{:S(2)}) copy-start(f32[2,8,768]{2,1,0:T(8,128)} %param.31) | copy-start | bytes 147460
  12.3 83.3 %copy-start.41 = (f32[2,8,768]{2,1,0:T(8,128)S(1)}, f32[2,8,768]{2,1,0:T(8,128)}, u32[]{:S(2)}) copy-start(f32[2,8,768]{2,1,0:T(8,128)} %param.30) | copy-start | bytes 147460
  12.3 83.4 %copy-start.19 = (bf16[2,512,768]{2,1,0:T(8,128)(2,1)S(1)}, bf16[2,512,768]{2,1,0:T(8,128)(2,1)}, u32[]{:S(2)}) copy-start(bf16[2,512,768]{2,1,0:T(8,128)(2,1)} %param.20) | copy-start | bytes 4718596
  12.3 248.5 %all-gather.27.cloned.1.call-start = ((), (), s32[]{:S(2)}) async-start(), calls=%async_computation.3 | async-start | bytes 4866048 | tf_op jit(solution)/shard_map/all_gather | solution.py:49
  14.2 307.2 %all-gather.29.cloned.1.call-start = ((), (), s32[]{:S(2)}) async-start(), calls=%async_computation.4 | async-start | bytes 3649536 | tf_op jit(solution)/shard_map/all_gather | solution.py:45
  14.8 362.4 %all-gather.31.cloned.1.call-start = ((), (), s32[]{:S(2)}) async-start(), calls=%async_computation.5 | async-start | bytes 1216512 | tf_op jit(solution)/shard_map/all_gather | solution.py:46
  15.4 428.7 %all-gather.33.cloned.1.call-start = ((), (), s32[]{:S(2)}) async-start(), calls=%async_computation.6 | async-start | bytes 4866048 | tf_op jit(solution)/shard_map/all_gather | solution.py:47
  16.1 493.4 %all-gather.35.cloned.1.call-start = ((), (), s32[]{:S(2)}) async-start(), calls=%async_computation.7 | async-start | bytes 4866048 | tf_op jit(solution)/shard_map/all_gather | solution.py:49
  16.9 887.4 %all-reduce.6.cloned.1.call-start = ((), (), s32[]{:S(2)}) async-start(), calls=%async_computation.8 | async-start | bytes 196608 | tf_op jit(solution)/shard_map/psum | solution.py:309
  95.5 165.2 %copy-start.67 = (f32[768]{0:T(1024)}, f32[768]{0:T(1024)S(1)}, u32[]{:S(2)}) copy-start(f32[768]{0:T(1024)S(1)} %get-tuple-element.178) | copy-start | bytes 9220
  95.5 50.3 %copy-start.78 = (s32[2]{0:T(128)S(1)}, s32[2]{0:T(128)}, u32[]{:S(2)}) copy-start(s32[2]{0:T(128)} %param.23) | copy-start | bytes 28
  95.5 50.4 %copy-start.75 = (s32[2,80]{1,0:T(2,128)S(1)}, s32[2,80]{1,0:T(2,128)}, u32[]{:S(2)}) copy-start(s32[2,80]{1,0:T(2,128)} %param.22) | copy-start | bytes 1924
  145.3 115.5 %copy-start.64 = (f32[3072]{0:T(1024)}, f32[3072]{0:T(1024)S(1)}, u32[]{:S(2)}) copy-start(f32[3072]{0:T(1024)S(1)} %convert_element_type.210) | copy-start | bytes 36868
  149.0 9.4 %copy-start.62 = (f32[2304]{0:T(1024)}, f32[2304]{0:T(1024)S(1)}, u32[]{:S(2)}) copy-start(f32[2304]{0:T(1024)S(1)} %get-tuple-element.255) | copy-start | bytes 27652
  188.3 72.4 %copy-start.6 = (f32[1024,768]{1,0:T(8,128)}, f32[1024,768]{1,0:T(8,128)S(1)}, u32[]{:S(2)}) copy-start(f32[1024,768]{1,0:T(8,128)S(1)} %get-tuple-element.259) | copy-start | bytes 9437188
  188.3 72.4 %copy-start.45 = (f32[1024]{0:T(1024)}, f32[1024]{0:T(1024)S(1)}, u32[]{:S(2)}) copy-start(f32[1024]{0:T(1024)S(1)} %broadcast_multiply_fusion.3) | copy-start | bytes 12292
  188.8 42.9 %copy-start.49 = (f32[1024]{0:T(1024)}, f32[1024]{0:T(1024)S(1)}, u32[]{:S(2)}) copy-start(f32[1024]{0:T(1024)S(1)} %multiply_reduce_fusion.11) | copy-start | bytes 12292
  188.9 71.9 %copy-start.55 = (f32[1024]{0:T(1024)}, f32[1024]{0:T(1024)S(1)}, u32[]{:S(2)}) copy-start(f32[1024]{0:T(1024)S(1)} %fusion.212) | copy-start | bytes 12292
  195.5 65.3 %copy-start.73 = (f32[768]{0:T(1024)S(1)}, f32[768]{0:T(1024)}, u32[]{:S(2)}) copy-start(f32[768]{0:T(1024)} %get-tuple-element.176) | copy-start | bytes 9220
  260.8 13.3 %copy-start.42 = (f32[768]{0:T(1024)S(1)}, f32[768]{0:T(1024)}, u32[]{:S(2)}) copy-start(f32[768]{0:T(1024)} %get-tuple-element.174) | copy-start | bytes 9220
  260.8 13.3 %copy-start.54 = (f32[768]{0:T(1024)S(1)}, f32[768]{0:T(1024)}, u32[]{:S(2)}) copy-start(f32[768]{0:T(1024)} %get-tuple-element.175) | copy-start | bytes 9220
  273.6 103.7 %copy-start.30 = (f32[1024]{0:T(1024)}, f32[1024]{0:T(1024)S(1)}, u32[]{:S(2)}) copy-start(f32[1024]{0:T(1024)S(1)} %broadcast_multiply_fusion.2) | copy-start | bytes 12292
  274.1 103.2 %copy-start.47 = (f32[1024]{0:T(1024)}, f32[1024]{0:T(1024)S(1)}, u32[]{:S(2)}) copy-start(f32[1024]{0:T(1024)S(1)} %fusion.213) | copy-start | bytes 12292
  274.7 46.8 %copy-start.61 = (f32[2304]{0:T(1024)S(1)}, f32[2304]{0:T(1024)}, u32[]{:S(2)}) copy-start(f32[2304]{0:T(1024)} %get-tuple-element.253) | copy-start | bytes 27652
  274.7 46.8 %copy-start.63 = (f32[2304]{0:T(1024)S(1)}, f32[2304]{0:T(1024)}, u32[]{:S(2)}) copy-start(f32[2304]{0:T(1024)} %copy-done.62) | copy-start | bytes 27652
  275.3 54.7 %copy-start.28 = (bf16[1024,16]{0,1:T(8,128)(2,1)}, bf16[1024,16]{0,1:T(8,128)(2,1)S(1)}, u32[]{:S(2)}) copy-start(bf16[1024,16]{0,1:T(8,128)(2,1)S(1)} %convolution_convert_fusion.2) | copy-start | bytes 98308
  336.8 40.5 %copy-start.72 = (f32[768]{0:T(1024)S(1)}, f32[768]{0:T(1024)}, u32[]{:S(2)}) copy-start(f32[768]{0:T(1024)} %get-tuple-element.171) | copy-start | bytes 9220
  355.3 22.0 %copy-start.20 = (bf16[2,512,768]{2,1,0:T(8,128)(2,1)}, bf16[2,512,768]{2,1,0:T(8,128)(2,1)S(1)}, u32[]{:S(2)}) copy-start(bf16[2,512,768]{2,1,0:T(8,128)(2,1)S(1)} %get-tuple-element.105) | copy-start | bytes 4718596
  377.2 66.8 %copy-start.66 = (f32[3072]{0:T(1024)S(1)}, f32[3072]{0:T(1024)}, u32[]{:S(2)}) copy-start(f32[3072]{0:T(1024)} %convert_element_type.211) | copy-start | bytes 36868
  377.2 66.8 %copy-start.69 = (f32[768]{0:T(1024)S(1)}, f32[768]{0:T(1024)}, u32[]{:S(2)}) copy-start(f32[768]{0:T(1024)} %get-tuple-element.170) | copy-start | bytes 9220
  377.3 66.8 %copy-start.71 = (f32[768]{0:T(1024)S(1)}, f32[768]{0:T(1024)}, u32[]{:S(2)}) copy-start(f32[768]{0:T(1024)} %get-tuple-element.169) | copy-start | bytes 9220
  444.1 65.4 %copy-start.70 = (f32[768]{0:T(1024)S(1)}, f32[768]{0:T(1024)}, u32[]{:S(2)}) copy-start(f32[768]{0:T(1024)} %get-tuple-element.168) | copy-start | bytes 9220
  509.5 12.6 %copy-start.4 = (f32[2,512,768]{2,1,0:T(8,128)S(1)}, f32[2,512,768]{2,1,0:T(8,128)}, u32[]{:S(2)}) copy-start(f32[2,512,768]{2,1,0:T(8,128)} %fusion.190) | copy-start | bytes 9437188
  509.5 12.6 %copy-start.44 = (f32[768]{0:T(1024)S(1)}, f32[768]{0:T(1024)}, u32[]{:S(2)}) copy-start(f32[768]{0:T(1024)} %get-tuple-element.166) | copy-start | bytes 9220
  558.2 83.9 %copy-start.29 = (bf16[1024,16]{0,1:T(8,128)(2,1)S(1)}, bf16[1024,16]{0,1:T(8,128)(2,1)}, u32[]{:S(2)}) copy-start(bf16[1024,16]{0,1:T(8,128)(2,1)} %copy-done.28) | copy-start | bytes 98308
  558.2 88.7 %copy-start.34 = (bf16[2,8,768]{2,1,0:T(8,128)(2,1)S(1)}, bf16[2,8,768]{2,1,0:T(8,128)(2,1)}, u32[]{:S(2)}) copy-start(bf16[2,8,768]{2,1,0:T(8,128)(2,1)} %copy-done.32) | copy-start | bytes 73732
  558.4 8.3 copy-start.22
  560.3 7.2 copy-start.13
  569.9 11.5 %slice-start = ((s8[12582912]{0:T(1024)(128)(4,1)}), s8[4194304]{0:T(1024)(128)(4,1)S(1)}, s32[]{:S(2)}) async-start(s8[12582912]{0:T(1024)(128)(4,1)} %bitcast.333), calls=%async_computation.9 | async-start | bytes 8388608 | tf_op jit(solution)/shard_map/while
  569.9 11.5 %slice-start.1 = ((s8[12582912]{0:T(1024)(128)(4,1)}), s8[4194304]{0:T(1024)(128)(4,1)S(1)}, s32[]{:S(2)}) async-start(s8[12582912]{0:T(1024)(128)(4,1)} %bitcast.333), calls=%async_computation.10 | async-start | bytes 8388608 | tf_op jit(solution)/shard_map/while
  569.9 11.6 %slice-start.2 = ((s8[12582912]{0:T(1024)(128)(4,1)}), s8[4194304]{0:T(1024)(128)(4,1)S(1)}, s32[]{:S(2)}) async-start(s8[12582912]{0:T(1024)(128)(4,1)} %bitcast.333), calls=%async_computation.11 | async-start | bytes 8388608 | tf_op jit(solution)/shard_map/while
  600.0 8.3 copy-start.22
  601.9 7.2 copy-start.13
  611.4 11.5 %slice-start = ((s8[12582912]{0:T(1024)(128)(4,1)}), s8[4194304]{0:T(1024)(128)(4,1)S(1)}, s32[]{:S(2)}) async-start(s8[12582912]{0:T(1024)(128)(4,1)} %bitcast.333), calls=%async_computation.9 | async-start | bytes 8388608 | tf_op jit(solution)/shard_map/while
  611.4 11.5 %slice-start.1 = ((s8[12582912]{0:T(1024)(128)(4,1)}), s8[4194304]{0:T(1024)(128)(4,1)S(1)}, s32[]{:S(2)}) async-start(s8[12582912]{0:T(1024)(128)(4,1)} %bitcast.333), calls=%async_computation.10 | async-start | bytes 8388608 | tf_op jit(solution)/shard_map/while
  611.4 11.6 %slice-start.2 = ((s8[12582912]{0:T(1024)(128)(4,1)}), s8[4194304]{0:T(1024)(128)(4,1)S(1)}, s32[]{:S(2)}) async-start(s8[12582912]{0:T(1024)(128)(4,1)} %bitcast.333), calls=%async_computation.11 | async-start | bytes 8388608 | tf_op jit(solution)/shard_map/while
  659.8 21.2 %copy-start.50 = (f32[1024]{0:T(1024)S(1)}, f32[1024]{0:T(1024)}, u32[]{:S(2)}) copy-start(f32[1024]{0:T(1024)} %copy-done.49) | copy-start | bytes 12292
  659.8 21.2 %copy-start.56 = (f32[1024]{0:T(1024)S(1)}, f32[1024]{0:T(1024)}, u32[]{:S(2)}) copy-start(f32[1024]{0:T(1024)} %copy-done.55) | copy-start | bytes 12292
  690.6 82.5 %copy-start.27 = (bf16[1024,16]{0,1:T(8,128)(2,1)S(1)}, bf16[1024,16]{0,1:T(8,128)(2,1)}, u32[]{:S(2)}) copy-start(bf16[1024,16]{0,1:T(8,128)(2,1)} %copy-done.26) | copy-start | bytes 98308
  690.6 87.2 %copy-start.39 = (bf16[2,8,768]{2,1,0:T(8,128)(2,1)S(1)}, bf16[2,8,768]{2,1,0:T(8,128)(2,1)}, u32[]{:S(2)}) copy-start(bf16[2,8,768]{2,1,0:T(8,128)(2,1)} %copy-done.36) | copy-start | bytes 73732
  701.3 11.6 %slice-start.3 = ((s8[12582912]{0:T(1024)(128)(4,1)}), s8[4194304]{0:T(1024)(128)(4,1)S(1)}, s32[]{:S(2)}) async-start(s8[12582912]{0:T(1024)(128)(4,1)} %bitcast.335), calls=%async_computation.12 | async-start | bytes 8388608 | tf_op jit(solution)/shard_map/while
  701.3 11.6 %slice-start.4 = ((s8[12582912]{0:T(1024)(128)(4,1)}), s8[4194304]{0:T(1024)(128)(4,1)S(1)}, s32[]{:S(2)}) async-start(s8[12582912]{0:T(1024)(128)(4,1)} %bitcast.335), calls=%async_computation.13 | async-start | bytes 8388608 | tf_op jit(solution)/shard_map/while
  701.4 12.0 %slice-start.5 = ((s8[12582912]{0:T(1024)(128)(4,1)}), s8[4194304]{0:T(1024)(128)(4,1)S(1)}, s32[]{:S(2)}) async-start(s8[12582912]{0:T(1024)(128)(4,1)} %bitcast.335), calls=%async_computation.14 | async-start | bytes 8388608 | tf_op jit(solution)/shard_map/while
  742.5 11.6 %slice-start.3 = ((s8[12582912]{0:T(1024)(128)(4,1)}), s8[4194304]{0:T(1024)(128)(4,1)S(1)}, s32[]{:S(2)}) async-start(s8[12582912]{0:T(1024)(128)(4,1)} %bitcast.335), calls=%async_computation.12 | async-start | bytes 8388608 | tf_op jit(solution)/shard_map/while
  742.5 11.6 %slice-start.4 = ((s8[12582912]{0:T(1024)(128)(4,1)}), s8[4194304]{0:T(1024)(128)(4,1)S(1)}, s32[]{:S(2)}) async-start(s8[12582912]{0:T(1024)(128)(4,1)} %bitcast.335), calls=%async_computation.13 | async-start | bytes 8388608 | tf_op jit(solution)/shard_map/while
  742.5 12.1 %slice-start.5 = ((s8[12582912]{0:T(1024)(128)(4,1)}), s8[4194304]{0:T(1024)(128)(4,1)S(1)}, s32[]{:S(2)}) async-start(s8[12582912]{0:T(1024)(128)(4,1)} %bitcast.335), calls=%async_computation.14 | async-start | bytes 8388608 | tf_op jit(solution)/shard_map/while
  781.7 7.0 copy-start.9
  781.7 7.0 copy-start.15
  781.7 7.0 copy-start.58
  781.7 124.0 %copy-start.1 = (bf16[2,80,768]{2,1,0:T(8,128)(2,1)S(1)}, bf16[2,80,768]{2,1,0:T(8,128)(2,1)}, u32[]{:S(2)}) copy-start(bf16[2,80,768]{2,1,0:T(8,128)(2,1)} %param.21) | copy-start | bytes 737284
  (40 other events, 161.6 us)
Sparse Core Ops, SparseCore 0:
  11.5 61.4 all-gather.20
  76.4 52.3 all-gather.22
  131.8 63.6 all-gather.24
  198.2 62.4 all-gather.26
  263.5 57.9 all-gather.28
  324.8 52.4 all-gather.30
  380.1 63.9 all-gather.32
  447.0 62.4 all-gather.34
  781.8 122.4 all-reduce.5
where the time goes:
time: 919 us; the launch traced here: 912 us
  matrix products  329 us (36%)
  waiting for transfers between devices  305 us (33%)
  blocking collectives  119 us (13%)
  local copies, waits for them, and re-layouts  87.3 us (9%)
  other arithmetic  53.9 us (6%)
  between operations  15 us (2%)
    dot_general x14, matrix products, matrix_multiply(): return jnp.dot(left, right, preferred_element_type=jnp.float32)  133 us
    psum x1, waiting for transfers between devices, on_device(): lax.psum((query_gradient_total, value_gradient_total), ('dp', 'fsdp'))  113 us
    all_gather x2, blocking collectives, fetch_forward(): lax.all_gather(layer_small, ('dp', 'fsdp'), axis=0, tiled=True)  73.5 us
    dot_general x12, matrix products, transposed_multiply(): lax.dot_general(left, right, (((1,), (1,)), ((), ())), preferred_element_...  72.1 us
    all_gather x2, waiting for transfers between devices, fetch_forward(): lax.all_gather(layer_in, ('dp', 'fsdp'), axis=0, tiled=True)  68.4 us
    all_gather x2, waiting for transfers between devices, fetch_forward(): lax.all_gather(layer_out, ('dp', 'fsdp'), axis=0, tiled=True)  57.8 us
    dot_general x4, matrix products, attend_back(): jnp.einsum('qhd,khd->hqk', grad_view, value_matrix_rows, preferred_elemen...  46.1 us
    unnamed x1, blocking collectives  45.6 us
  transfers between devices with their start and end apart: 9, of which 7 were waited for; matrix products, arithmetic and copies ran while one was open for 21% of the time, Pallas kernels for 0%

commit v1 on v0

--- a/solution.py
+++ b/solution.py
@@ -307,7 +307,7 @@
             value_up_weight[layer_index],
         )
         query_gradient_total, value_gradient_total = lax.psum(
-            (query_gradient_total, value_gradient_total), ("dp", "fsdp")
+            lax.psum((query_gradient_total, value_gradient_total), axis_name="fsdp"), axis_name="dp"
         )
         query_gradient_stack[layer_index] = query_gradient_total
         value_gradient_stack[layer_index] = value_gradient_total

time: 919 us -> 924 us (level)
    psum x1 -> x2, waiting for transfers between devices: 113 us -> 112 us  [the longest x1 107 us: on_device(): lax.psum(lax.psum((query_gradient_total, value_gradient_total), axis_name...]
  transfers between devices with their start and end apart: 9 -> 10, of which waited for: 7 -> 8; matrix products, arithmetic and copies ran while one was open for 21% -> 22% of each run, Pallas kernels for 0% -> 0%
where the time goes in v1:
time: 924 us; the launch traced here: 916 us
  matrix products  333 us (36%)
  waiting for transfers between devices  305 us (33%)
  blocking collectives  119 us (13%)
  local copies, waits for them, and re-layouts  86.9 us (9%)
  other arithmetic  54 us (6%)
  between operations  15.3 us (2%)
    dot_general x14, matrix products, matrix_multiply(): return jnp.dot(left, right, preferred_element_type=jnp.float32)  133 us
    psum x1, waiting for transfers between devices, on_device(): lax.psum(lax.psum((query_gradient_total, value_gradient_total), axis_name...  107 us
    dot_general x12, matrix products, transposed_multiply(): lax.dot_general(left, right, (((1,), (1,)), ((), ())), preferred_element_...  76 us
    all_gather x2, blocking collectives, fetch_forward(): lax.all_gather(layer_small, ('dp', 'fsdp'), axis=0, tiled=True)  73.5 us
    all_gather x2, waiting for transfers between devices, fetch_forward(): lax.all_gather(layer_in, ('dp', 'fsdp'), axis=0, tiled=True)  68.5 us
    all_gather x2, waiting for transfers between devices, fetch_forward(): lax.all_gather(layer_out, ('dp', 'fsdp'), axis=0, tiled=True)  57.9 us
    dot_general x4, matrix products, attend_back(): jnp.einsum('qhd,khd->hqk', grad_view, value_matrix_rows, preferred_elemen...  46 us
    unnamed x1, blocking collectives  45.4 us
  transfers between devices with their start and end apart: 10, of which 8 were waited for; matrix products, arithmetic and copies ran while one was open for 22% of the time, Pallas kernels for 0%

profile of v1, /device:TPU:8, one launch (start us, length us, event | category | flops | bytes accessed | tf_op | source)
XLA Modules:
  0.0 916.0 jit_solution(5538297534358250238)
XLA Ops:
  17.6 36.0 %all-gather.7 = bf16[1,768,24]{2,1,0:T(8,128)(2,1)S(1)} all-gather(bf16[1,24,24]{2,1,0:T(8,128)(2,1)S(1)} %get-tuple-element.253), channel_id=9, replica_groups=mesh['dp'=16,'fsdp'=2] {'dp','fsdp'}, dimensions={1}, use_global_device_ids=true | all-gather | bytes 38016 | tf_op jit(solution)/shard_map/all_gather | solution.py:50
  56.4 37.5 %all-gather.1 = bf16[1,768,24]{2,1,0:T(8,128)(2,1)S(1)} all-gather(bf16[1,24,24]{2,1,0:T(8,128)(2,1)S(1)} %get-tuple-element.254), channel_id=3, replica_groups=mesh['dp'=16,'fsdp'=2] {'dp','fsdp'}, dimensions={1}, use_global_device_ids=true | all-gather | bytes 38016 | tf_op jit(solution)/shard_map/all_gather | solution.py:50
  99.7 45.4 %all-reduce.4 = (bf16[3072]{0:T(1024)(128)(2,1)S(1)}, bf16[3072]{0:T(1024)(128)(2,1)S(1)}) all-reduce(bf16[3072]{0:T(1024)(128)(2,1)S(1)} %dynamic-update-slice, bf16[3072]{0:T(1024)(128)(2,1)S(1)} %dynamic-update-slice.1), channel_id=6, replica_groups=mesh['dp'=16,'fsdp'=2] {'dp','fsdp'}, use_global_device_ids=true, to_apply=%add | all-reduce | flops 6144 | bytes 24576
  148.9 9.4 %fusion.54 = bf16[1024,2304]{1,0:T(8,128)(2,1)} fusion(f32[1024,768]{1,0:T(8,128)S(1)} %convolution_multiply_fusion.2, f32[1024,768]{1,0:T(8,128)} %convolution_multiply_fusion.3, bf16[1024,768]{1,0:T(8,128)(2,1)} %bitcast.373, f32[2304]{0:T(1024)S(1)} %get-tuple-element.259, f32[2304]{0:T(1024)S(1)} %get-tuple-element.258, ...), kind=kOutput, calls=%fused_computation.111 | convolution fusion | flops 3635675136 | bytes 16140288 | tf_op jit(solution)/shard_map/dot_general | solution.py:28
  158.3 6.7 copy.66
  165.1 18.2 %while.44 = (s32[]{:T(128)}, bf16[2,512,768]{2,1,0:T(8,128)(2,1)S(1)}, f32[2,12,512]{2,1,0:T(8,128)S(1)}, bf16[2,512,2304]{1,2,0:T(8,128)(2,1)}, s32[]{:T(128)}) while((s32[]{:T(128)}, bf16[2,512,768]{2,1,0:T(8,128)(2,1)S(1)}, f32[2,12,512]{2,1,0:T(8,128)S(1)}, bf16[2,512,2304]{1,2,0:T(8,128)(2,1)}, s32[]{:T(128)}) %tuple.124), condition=%wide.region_3.4_spmd, body=%wide.region_0.3_spmd.sunk | while | flops 834004992 | bytes 48996424 | solution.py:150
  170.9 2.8 fusion.271
  179.9 2.8 fusion.271
  184.4 3.8 fusion.223
  188.8 6.7 all-gather.25.cloned.1.call-done
  195.5 36.2 %fusion.42 = (f32[1024,3072]{1,0:T(8,128)}, f32[1024,3072]{1,0:T(8,128)}) fusion(f32[3072]{0:T(1024)S(1)} %convert_element_type.210, bf16[1,768,3072]{2,1,0:T(8,128)(2,1)} %all-gather.25.cloned.1.call-done, f32[1024,768]{1,0:T(8,128)S(1)} %get-tuple-element.263, f32[768]{0:T(1024)S(1)} %get-tuple-element.177, f32[768]{0:T(1024)S(1)} %get-tuple-element.178, ...), kind=kOutput, calls=%fused_computation.78 | convolution fusion | flops 5033951232 | bytes 33056768 | tf_op jit(solution)/shard_map/dot_general | solution.py:28
  231.8 29.0 %all-gather.27.cloned.1.call-done = bf16[1,3072,768]{2,1,0:T(8,128)(2,1)} async-done(((bf16[1,96,768]{2,1,0:T(8,128)(2,1)}), bf16[1,3072,768]{2,1,0:T(8,128)(2,1)}) %all-gather.27.cloned.1.call-update) | async-done | bytes 4718608 | tf_op jit(solution)/shard_map/all_gather | solution.py:49
  260.8 12.7 %fusion.224 = (f32[1024]{0:T(1024)S(1)}, f32[1024,768]{1,0:T(8,128)S(1)}) fusion(f32[768]{0:T(1024)S(1)} %copy-done.72, bf16[1,3072,768]{2,1,0:T(8,128)(2,1)} %all-gather.27.cloned.1.call-done, f32[1024,3072]{1,0:T(8,128)} %get-tuple-element.264, f32[1024,3072]{1,0:T(8,128)} %get-tuple-element.265, f32[3072]{0:T(1024)S(1)} %convert_element_type.210, ...), kind=kOutput, calls=%fused_computation.316 | convolution fusion | flops 4849925120 | bytes 36209664 | tf_op jit(solution)/shard_map/dot_general | solution.py:28
  279.9 41.6 %all-gather.29.cloned.1.call-done = bf16[1,768,2304]{2,1,0:T(8,128)(2,1)} async-done(((bf16[1,24,2304]{2,1,0:T(8,128)(2,1)}), bf16[1,768,2304]{2,1,0:T(8,128)(2,1)}) %all-gather.29.cloned.1.call-update) | async-done | bytes 3538960 | tf_op jit(solution)/shard_map/all_gather | solution.py:45
  321.5 8.5 fusion.55
  330.0 6.7 copy.70
  336.8 18.5 %while.45 = (s32[]{:T(128)}, bf16[2,512,768]{2,1,0:T(8,128)(2,1)S(1)}, f32[2,12,512]{2,1,0:T(8,128)S(1)}, bf16[2,512,2304]{1,2,0:T(8,128)(2,1)}, s32[]{:T(128)}) while((s32[]{:T(128)}, bf16[2,512,768]{2,1,0:T(8,128)(2,1)S(1)}, f32[2,12,512]{2,1,0:T(8,128)S(1)}, bf16[2,512,2304]{1,2,0:T(8,128)(2,1)}, s32[]{:T(128)}) %tuple.127), condition=%wide.region_11.12_spmd, body=%wide.region_8.11_spmd.sunk | while | flops 834004992 | bytes 48996424 | solution.py:150
  343.1 2.8 fusion.273
  352.1 2.8 fusion.273
  355.3 22.0 %all-gather.31.cloned.1.call-done = bf16[1,768,768]{2,1,0:T(8,128)(2,1)} async-done(((bf16[1,24,768]{2,1,0:T(8,128)(2,1)}), bf16[1,768,768]{2,1,0:T(8,128)(2,1)}) %all-gather.31.cloned.1.call-update) | async-done | bytes 1179664 | tf_op jit(solution)/shard_map/all_gather | solution.py:46
  377.3 4.5 fusion.225
  382.3 61.8 %all-gather.33.cloned.1.call-done = bf16[1,768,3072]{2,1,0:T(8,128)(2,1)} async-done(((bf16[1,24,3072]{2,1,0:T(8,128)(2,1)}), bf16[1,768,3072]{2,1,0:T(8,128)(2,1)}) %all-gather.33.cloned.1.call-update) | async-done | bytes 4718608 | tf_op jit(solution)/shard_map/all_gather | solution.py:47
  444.1 36.5 %fusion.43 = (f32[1024,3072]{1,0:T(8,128)}, f32[1024,3072]{1,0:T(8,128)}) fusion(f32[3072]{0:T(1024)S(1)} %copy-done.65, bf16[1,768,3072]{2,1,0:T(8,128)(2,1)} %all-gather.33.cloned.1.call-done, f32[1024,768]{1,0:T(8,128)S(1)} %get-tuple-element.269, f32[768]{0:T(1024)S(1)} %copy-done.70, f32[768]{0:T(1024)S(1)} %copy-done.68, f32[1024]{0:T(1024)S(1)} %fusion.202, ...), kind=kOutput, calls=%fused_computation.79 | convolution fusion | flops 5033951232 | bytes 33056768 | tf_op jit(solution)/shard_map/dot_general | solution.py:28
  480.7 28.9 %all-gather.35.cloned.1.call-done = bf16[1,3072,768]{2,1,0:T(8,128)(2,1)} async-done(((bf16[1,96,768]{2,1,0:T(8,128)(2,1)}), bf16[1,3072,768]{2,1,0:T(8,128)(2,1)}) %all-gather.35.cloned.1.call-update) | async-done | bytes 4718608 | tf_op jit(solution)/shard_map/all_gather | solution.py:49
  509.5 12.6 %fusion.226 = (f32[1024]{0:T(1024)S(1)}, f32[1024,768]{1,0:T(8,128)S(1)}) fusion(f32[768]{0:T(1024)S(1)} %copy-done.69, bf16[1,3072,768]{2,1,0:T(8,128)(2,1)} %all-gather.35.cloned.1.call-done, f32[1024,3072]{1,0:T(8,128)} %get-tuple-element.270, f32[1024,3072]{1,0:T(8,128)} %get-tuple-element.271, f32[3072]{0:T(1024)S(1)} %copy-done.65, ...), kind=kOutput, calls=%fused_computation.318 | convolution fusion | flops 4849925120 | bytes 36209664 | tf_op jit(solution)/shard_map/dot_general | solution.py:28
  523.0 3.4 fusion.217
  526.4 22.2 %multiply_reduce_fusion.6 = (f32[1024]{0:T(1024)S(1)}, f32[1024,768]{1,0:T(8,128)}) fusion(f32[1024,768]{1,0:T(8,128)S(1)} %get-tuple-element.269, f32[1024]{0:T(1024)S(1)} %broadcast_multiply_fusion.1, f32[768]{0:T(1024)S(1)} %copy-done.68, bf16[1,768,3072]{2,1,0:T(8,128)(2,1)} %all-gather.33.cloned.1.call-done, f32[1024,3072]{1,0:T(8,128)} %get-tuple-element.270, ...), kind=kOutput, calls=%fused_computation.150 | convolution fusion | flops 9717152768 | bytes 44067840 | tf_op jit(solution)/shard_map/dot_general | solution.py:32
  548.7 2.8 fusion.216
  553.1 2.6 convolution_convert_fusion.1
  555.8 2.5 broadcast.342.clone2
  558.2 83.9 %while.46 = (s32[]{:T(128)}, bf16[2,512,2304]{2,1,0:T(8,128)(2,1)}, bf16[2,512,2304]{1,2,0:T(8,128)(2,1)}, f32[2,12,512]{2,1,0:T(8,128)S(1)}, bf16[2,512,768]{2,1,0:T(8,128)(2,1)}, /*index=5*/s32[]{:T(128)}) while((s32[]{:T(128)}, bf16[2,512,2304]{2,1,0:T(8,128)(2,1)}, bf16[2,512,2304]{1,2,0:T(8,128)(2,1)}, f32[2,12,512]{2,1,0:T(8,128)S(1)}, ...), condition=%wide.region_22.23_spmd, body=%wide.region_20.22_spmd.sunk | while | flops 2055333888 | bytes 168870656 | solution.py:214
  560.3 6.4 fusion.279
  569.9 11.5 %multiply_reduce_fusion.18 = (f32[12,512]{1,0:T(8,128)S(1)}, f32[12,512,512]{1,2,0:T(8,128)}) fusion(f32[12,512,512]{1,2,0:T(8,128)} %fusion.279, f32[12,512]{1,0:T(8,128)S(1)} %dynamic-slice_bitcast_fusion.4, bf16[512,12,64]{0,2,1:T(8,128)(2,1)S(1)} %bitcast.343, bf16[512,3,12,64]{0,3,2,1:T(8,128)(2,1)S(1)} %bitcast.334), kind=kOutput, calls=%fused_computation.29.clone.1 | convolution fusion | flops 415229952 | bytes 26796032 | tf_op jit(solution)/shard_map/while/body/eval_jaxpr/qhd,khd->hqk/dot_general | solution.py:97
  581.5 6.9 multiply_convert_fusion.16
  591.5 2.4 fusion.280
  594.3 2.6 copy.109
  596.8 3.2 constant_dynamic-update-slice_fusion.10
  601.9 6.4 fusion.279
  611.5 11.5 %multiply_reduce_fusion.18 = (f32[12,512]{1,0:T(8,128)S(1)}, f32[12,512,512]{1,2,0:T(8,128)}) fusion(f32[12,512,512]{1,2,0:T(8,128)} %fusion.279, f32[12,512]{1,0:T(8,128)S(1)} %dynamic-slice_bitcast_fusion.4, bf16[512,12,64]{0,2,1:T(8,128)(2,1)S(1)} %bitcast.343, bf16[512,3,12,64]{0,3,2,1:T(8,128)(2,1)S(1)} %bitcast.334), kind=kOutput, calls=%fused_computation.29.clone.1 | convolution fusion | flops 415229952 | bytes 26796032 | tf_op jit(solution)/shard_map/while/body/eval_jaxpr/qhd,khd->hqk/dot_general | solution.py:97
  623.1 6.9 multiply_convert_fusion.16
  633.1 2.4 fusion.280
  635.8 2.6 copy.109
  638.4 3.3 constant_dynamic-update-slice_fusion.10
  642.1 2.5 fusion.168
  649.4 6.0 fusion.84
  659.8 21.1 %multiply_reduce_fusion.4 = (f32[1024]{0:T(1024)S(1)}, f32[1024,768]{1,0:T(8,128)}) fusion(f32[1024,768]{1,0:T(8,128)S(1)} %copy-done.7, f32[1024]{0:T(1024)S(1)} %copy-done.45, f32[768]{0:T(1024)S(1)} %copy-done.67, bf16[1,768,3072]{2,1,0:T(8,128)(2,1)} %all-gather.25.cloned.1.call-done, f32[1024,3072]{1,0:T(8,128)} %get-tuple-element.264, ...), kind=kOutput, calls=%fused_computation.146 | convolution fusion | flops 9717152768 | bytes 44067840 | tf_op jit(solution)/shard_map/dot_general | solution.py:32
  680.9 2.8 fusion.214
  685.3 2.7 convolution_convert_fusion
  688.0 2.5 broadcast.342.clone
  690.5 82.1 %while.47 = (s32[]{:T(128)}, bf16[2,512,2304]{2,1,0:T(8,128)(2,1)}, bf16[2,512,2304]{1,2,0:T(8,128)(2,1)}, f32[2,12,512]{2,1,0:T(8,128)S(1)}, bf16[2,512,768]{2,1,0:T(8,128)(2,1)}, /*index=5*/s32[]{:T(128)}) while((s32[]{:T(128)}, bf16[2,512,2304]{2,1,0:T(8,128)(2,1)}, bf16[2,512,2304]{1,2,0:T(8,128)(2,1)}, f32[2,12,512]{2,1,0:T(8,128)S(1)}, ...), condition=%wide.region_29.30_spmd, body=%wide.region_27.29_spmd.sunk | while | flops 2055333888 | bytes 168477376 | solution.py:214
  692.5 6.3 fusion.288
  701.2 11.5 %multiply_reduce_fusion.19 = (f32[12,512]{1,0:T(8,128)S(1)}, f32[12,512,512]{1,2,0:T(8,128)}) fusion(f32[12,512,512]{1,2,0:T(8,128)} %fusion.288, f32[12,512]{1,0:T(8,128)S(1)} %dynamic-slice_bitcast_fusion.5, bf16[512,12,64]{0,2,1:T(8,128)(2,1)S(1)} %bitcast.345, bf16[512,3,12,64]{0,3,2,1:T(8,128)(2,1)S(1)} %bitcast.338), kind=kOutput, calls=%fused_computation.53.clone.1 | convolution fusion | flops 415229952 | bytes 26796032 | tf_op jit(solution)/shard_map/while/body/eval_jaxpr/qhd,khd->hqk/dot_general | solution.py:97
  713.2 6.9 multiply_convert_fusion.17
  725.9 2.4 copy.111
  728.3 3.3 constant_dynamic-update-slice_fusion.11
  733.4 6.3 fusion.288
  742.2 11.5 %multiply_reduce_fusion.19 = (f32[12,512]{1,0:T(8,128)S(1)}, f32[12,512,512]{1,2,0:T(8,128)}) fusion(f32[12,512,512]{1,2,0:T(8,128)} %fusion.288, f32[12,512]{1,0:T(8,128)S(1)} %dynamic-slice_bitcast_fusion.5, bf16[512,12,64]{0,2,1:T(8,128)(2,1)S(1)} %bitcast.345, bf16[512,3,12,64]{0,3,2,1:T(8,128)(2,1)S(1)} %bitcast.338), kind=kOutput, calls=%fused_computation.53.clone.1 | convolution fusion | flops 415229952 | bytes 26796032 | tf_op jit(solution)/shard_map/while/body/eval_jaxpr/qhd,khd->hqk/dot_general | solution.py:97
  754.1 6.9 multiply_convert_fusion.17
  766.8 2.4 copy.111
  769.3 3.3 constant_dynamic-update-slice_fusion.11
  779.5 9.1 fusion.87
  790.5 5.6 all-reduce.10.cloned.1.call-done
  796.1 4.6 add_add_fusion.4
  800.7 106.9 %all-reduce.8.cloned.1.call-done = (f32[1,8,768]{2,1,0:T(8,128)}, f32[1,8,768]{2,1,0:T(8,128)}, f32[1,8,768]{2,1,0:T(8,128)}, f32[1,8,768]{2,1,0:T(8,128)}) async-done(((f32[1,8,768]{2,1,0:T(8,128)}, f32[1,8,768]{2,1,0:T(8,128)}, f32[1,8,768]{2,1,0:T(8,128)}, f32[1,8,768]{2,1,0:T(8,128)}), (f32[1,8,768]{2,1,0:T(8,128)}, f32[1,8,768]{2,1,0:T(8,128)}, f32[1,8,768]{2,1,0:T(8,128)}, ...) | async-done | bytes 98320 | tf_op jit(solution)/shard_map/psum | solution.py:309
  (330 shorter events, 116.8 us)
Async XLA Ops:
  7.2 138.7 %copy-start = (bf16[2,80,768]{2,1,0:T(8,128)(2,1)S(1)}, bf16[2,80,768]{2,1,0:T(8,128)(2,1)}, u32[]{:S(2)}) copy-start(bf16[2,80,768]{2,1,0:T(8,128)(2,1)} %param.21) | copy-start | bytes 737284
  7.2 141.7 %all-gather.21.cloned.1.call-start = ((), (), s32[]{:S(2)}) async-start(), calls=%async_computation | async-start | bytes 3649536 | tf_op jit(solution)/shard_map/all_gather | solution.py:45
  9.0 174.4 %all-gather.23.cloned.1.call-start = ((), (), s32[]{:S(2)}) async-start(), calls=%async_computation.1 | async-start | bytes 1216512 | tf_op jit(solution)/shard_map/all_gather | solution.py:46
  10.5 185.1 %all-gather.25.cloned.1.call-start = ((), (), s32[]{:S(2)}) async-start(), calls=%async_computation.2 | async-start | bytes 4866048 | tf_op jit(solution)/shard_map/all_gather | solution.py:47
  12.3 83.4 %copy-start.39 = (f32[2,8,768]{2,1,0:T(8,128)S(1)}, f32[2,8,768]{2,1,0:T(8,128)}, u32[]{:S(2)}) copy-start(f32[2,8,768]{2,1,0:T(8,128)} %param.31) | copy-start | bytes 147460
  12.3 83.4 %copy-start.40 = (f32[2,8,768]{2,1,0:T(8,128)S(1)}, f32[2,8,768]{2,1,0:T(8,128)}, u32[]{:S(2)}) copy-start(f32[2,8,768]{2,1,0:T(8,128)} %param.30) | copy-start | bytes 147460
  12.3 83.4 %copy-start.18 = (bf16[2,512,768]{2,1,0:T(8,128)(2,1)S(1)}, bf16[2,512,768]{2,1,0:T(8,128)(2,1)}, u32[]{:S(2)}) copy-start(bf16[2,512,768]{2,1,0:T(8,128)(2,1)} %param.20) | copy-start | bytes 4718596
  12.3 248.5 %all-gather.27.cloned.1.call-start = ((), (), s32[]{:S(2)}) async-start(), calls=%async_computation.3 | async-start | bytes 4866048 | tf_op jit(solution)/shard_map/all_gather | solution.py:49
  14.2 307.3 %all-gather.29.cloned.1.call-start = ((), (), s32[]{:S(2)}) async-start(), calls=%async_computation.4 | async-start | bytes 3649536 | tf_op jit(solution)/shard_map/all_gather | solution.py:45
  14.8 362.5 %all-gather.31.cloned.1.call-start = ((), (), s32[]{:S(2)}) async-start(), calls=%async_computation.5 | async-start | bytes 1216512 | tf_op jit(solution)/shard_map/all_gather | solution.py:46
  15.4 428.7 %all-gather.33.cloned.1.call-start = ((), (), s32[]{:S(2)}) async-start(), calls=%async_computation.6 | async-start | bytes 4866048 | tf_op jit(solution)/shard_map/all_gather | solution.py:47
  16.1 493.4 %all-gather.35.cloned.1.call-start = ((), (), s32[]{:S(2)}) async-start(), calls=%async_computation.7 | async-start | bytes 4866048 | tf_op jit(solution)/shard_map/all_gather | solution.py:49
  16.9 779.2 %all-reduce.10.cloned.1.call-start = ((), (), s32[]{:S(2)}) async-start(), calls=%async_computation.9 | async-start | bytes 196608 | tf_op jit(solution)/shard_map/psum | solution.py:310
  95.6 165.2 %copy-start.66 = (f32[768]{0:T(1024)}, f32[768]{0:T(1024)S(1)}, u32[]{:S(2)}) copy-start(f32[768]{0:T(1024)S(1)} %get-tuple-element.178) | copy-start | bytes 9220
  95.6 50.2 %copy-start.77 = (s32[2]{0:T(128)S(1)}, s32[2]{0:T(128)}, u32[]{:S(2)}) copy-start(s32[2]{0:T(128)} %param.23) | copy-start | bytes 28
  95.6 50.3 %copy-start.74 = (s32[2,80]{1,0:T(2,128)S(1)}, s32[2,80]{1,0:T(2,128)}, u32[]{:S(2)}) copy-start(s32[2,80]{1,0:T(2,128)} %param.22) | copy-start | bytes 1924
  145.2 115.6 %copy-start.63 = (f32[3072]{0:T(1024)}, f32[3072]{0:T(1024)S(1)}, u32[]{:S(2)}) copy-start(f32[3072]{0:T(1024)S(1)} %convert_element_type.210) | copy-start | bytes 36868
  148.9 9.4 %copy-start.61 = (f32[2304]{0:T(1024)}, f32[2304]{0:T(1024)S(1)}, u32[]{:S(2)}) copy-start(f32[2304]{0:T(1024)S(1)} %get-tuple-element.259) | copy-start | bytes 27652
  188.3 72.5 %copy-start.6 = (f32[1024,768]{1,0:T(8,128)}, f32[1024,768]{1,0:T(8,128)S(1)}, u32[]{:S(2)}) copy-start(f32[1024,768]{1,0:T(8,128)S(1)} %get-tuple-element.263) | copy-start | bytes 9437188
  188.3 72.5 %copy-start.44 = (f32[1024]{0:T(1024)}, f32[1024]{0:T(1024)S(1)}, u32[]{:S(2)}) copy-start(f32[1024]{0:T(1024)S(1)} %broadcast_multiply_fusion.3) | copy-start | bytes 12292
  188.8 43.0 %copy-start.48 = (f32[1024]{0:T(1024)}, f32[1024]{0:T(1024)S(1)}, u32[]{:S(2)}) copy-start(f32[1024]{0:T(1024)S(1)} %multiply_reduce_fusion.11) | copy-start | bytes 12292
  188.8 72.0 %copy-start.54 = (f32[1024]{0:T(1024)}, f32[1024]{0:T(1024)S(1)}, u32[]{:S(2)}) copy-start(f32[1024]{0:T(1024)S(1)} %fusion.200) | copy-start | bytes 12292
  195.5 65.3 %copy-start.72 = (f32[768]{0:T(1024)S(1)}, f32[768]{0:T(1024)}, u32[]{:S(2)}) copy-start(f32[768]{0:T(1024)} %get-tuple-element.176) | copy-start | bytes 9220
  260.8 13.3 %copy-start.41 = (f32[768]{0:T(1024)S(1)}, f32[768]{0:T(1024)}, u32[]{:S(2)}) copy-start(f32[768]{0:T(1024)} %get-tuple-element.174) | copy-start | bytes 9220
  260.8 13.3 %copy-start.53 = (f32[768]{0:T(1024)S(1)}, f32[768]{0:T(1024)}, u32[]{:S(2)}) copy-start(f32[768]{0:T(1024)} %get-tuple-element.175) | copy-start | bytes 9220
  273.6 103.7 %copy-start.29 = (f32[1024]{0:T(1024)}, f32[1024]{0:T(1024)S(1)}, u32[]{:S(2)}) copy-start(f32[1024]{0:T(1024)S(1)} %broadcast_multiply_fusion.2) | copy-start | bytes 12292
  274.1 103.2 %copy-start.46 = (f32[1024]{0:T(1024)}, f32[1024]{0:T(1024)S(1)}, u32[]{:S(2)}) copy-start(f32[1024]{0:T(1024)S(1)} %fusion.201) | copy-start | bytes 12292
  274.7 46.8 %copy-start.60 = (f32[2304]{0:T(1024)S(1)}, f32[2304]{0:T(1024)}, u32[]{:S(2)}) copy-start(f32[2304]{0:T(1024)} %get-tuple-element.257) | copy-start | bytes 27652
  274.7 46.7 %copy-start.62 = (f32[2304]{0:T(1024)S(1)}, f32[2304]{0:T(1024)}, u32[]{:S(2)}) copy-start(f32[2304]{0:T(1024)} %copy-done.61) | copy-start | bytes 27652
  275.3 54.7 %copy-start.27 = (bf16[1024,16]{0,1:T(8,128)(2,1)}, bf16[1024,16]{0,1:T(8,128)(2,1)S(1)}, u32[]{:S(2)}) copy-start(bf16[1024,16]{0,1:T(8,128)(2,1)S(1)} %convolution_convert_fusion.2) | copy-start | bytes 98308
  336.8 40.5 %copy-start.71 = (f32[768]{0:T(1024)S(1)}, f32[768]{0:T(1024)}, u32[]{:S(2)}) copy-start(f32[768]{0:T(1024)} %get-tuple-element.171) | copy-start | bytes 9220
  355.3 22.0 %copy-start.19 = (bf16[2,512,768]{2,1,0:T(8,128)(2,1)}, bf16[2,512,768]{2,1,0:T(8,128)(2,1)S(1)}, u32[]{:S(2)}) copy-start(bf16[2,512,768]{2,1,0:T(8,128)(2,1)S(1)} %get-tuple-element.105) | copy-start | bytes 4718596
  377.3 66.8 %copy-start.65 = (f32[3072]{0:T(1024)S(1)}, f32[3072]{0:T(1024)}, u32[]{:S(2)}) copy-start(f32[3072]{0:T(1024)} %convert_element_type.211) | copy-start | bytes 36868
  377.3 66.8 %copy-start.68 = (f32[768]{0:T(1024)S(1)}, f32[768]{0:T(1024)}, u32[]{:S(2)}) copy-start(f32[768]{0:T(1024)} %get-tuple-element.170) | copy-start | bytes 9220
  377.3 66.8 %copy-start.70 = (f32[768]{0:T(1024)S(1)}, f32[768]{0:T(1024)}, u32[]{:S(2)}) copy-start(f32[768]{0:T(1024)} %get-tuple-element.169) | copy-start | bytes 9220
  444.1 65.4 %copy-start.69 = (f32[768]{0:T(1024)S(1)}, f32[768]{0:T(1024)}, u32[]{:S(2)}) copy-start(f32[768]{0:T(1024)} %get-tuple-element.168) | copy-start | bytes 9220
  509.5 12.6 %copy-start.4 = (f32[2,512,768]{2,1,0:T(8,128)S(1)}, f32[2,512,768]{2,1,0:T(8,128)}, u32[]{:S(2)}) copy-start(f32[2,512,768]{2,1,0:T(8,128)} %fusion.178) | copy-start | bytes 9437188
  509.5 12.6 %copy-start.43 = (f32[768]{0:T(1024)S(1)}, f32[768]{0:T(1024)}, u32[]{:S(2)}) copy-start(f32[768]{0:T(1024)} %get-tuple-element.166) | copy-start | bytes 9220
  558.2 83.9 %copy-start.28 = (bf16[1024,16]{0,1:T(8,128)(2,1)S(1)}, bf16[1024,16]{0,1:T(8,128)(2,1)}, u32[]{:S(2)}) copy-start(bf16[1024,16]{0,1:T(8,128)(2,1)} %copy-done.27) | copy-start | bytes 98308
  558.2 88.7 %copy-start.33 = (bf16[2,8,768]{2,1,0:T(8,128)(2,1)S(1)}, bf16[2,8,768]{2,1,0:T(8,128)(2,1)}, u32[]{:S(2)}) copy-start(bf16[2,8,768]{2,1,0:T(8,128)(2,1)} %copy-done.31) | copy-start | bytes 73732
  558.5 8.3 copy-start.21
  569.9 11.5 %slice-start = ((s8[12582912]{0:T(1024)(128)(4,1)}), s8[4194304]{0:T(1024)(128)(4,1)S(1)}, s32[]{:S(2)}) async-start(s8[12582912]{0:T(1024)(128)(4,1)} %bitcast.329), calls=%async_computation.10 | async-start | bytes 8388608 | tf_op jit(solution)/shard_map/while
  569.9 11.5 %slice-start.1 = ((s8[12582912]{0:T(1024)(128)(4,1)}), s8[4194304]{0:T(1024)(128)(4,1)S(1)}, s32[]{:S(2)}) async-start(s8[12582912]{0:T(1024)(128)(4,1)} %bitcast.329), calls=%async_computation.11 | async-start | bytes 8388608 | tf_op jit(solution)/shard_map/while
  569.9 11.6 %slice-start.2 = ((s8[12582912]{0:T(1024)(128)(4,1)}), s8[4194304]{0:T(1024)(128)(4,1)S(1)}, s32[]{:S(2)}) async-start(s8[12582912]{0:T(1024)(128)(4,1)} %bitcast.329), calls=%async_computation.12 | async-start | bytes 8388608 | tf_op jit(solution)/shard_map/while
  600.0 8.3 copy-start.21
  601.9 7.2 copy-start.13
  611.4 11.5 %slice-start = ((s8[12582912]{0:T(1024)(128)(4,1)}), s8[4194304]{0:T(1024)(128)(4,1)S(1)}, s32[]{:S(2)}) async-start(s8[12582912]{0:T(1024)(128)(4,1)} %bitcast.329), calls=%async_computation.10 | async-start | bytes 8388608 | tf_op jit(solution)/shard_map/while
  611.4 11.5 %slice-start.1 = ((s8[12582912]{0:T(1024)(128)(4,1)}), s8[4194304]{0:T(1024)(128)(4,1)S(1)}, s32[]{:S(2)}) async-start(s8[12582912]{0:T(1024)(128)(4,1)} %bitcast.329), calls=%async_computation.11 | async-start | bytes 8388608 | tf_op jit(solution)/shard_map/while
  611.5 11.6 %slice-start.2 = ((s8[12582912]{0:T(1024)(128)(4,1)}), s8[4194304]{0:T(1024)(128)(4,1)S(1)}, s32[]{:S(2)}) async-start(s8[12582912]{0:T(1024)(128)(4,1)} %bitcast.329), calls=%async_computation.12 | async-start | bytes 8388608 | tf_op jit(solution)/shard_map/while
  659.8 21.1 %copy-start.49 = (f32[1024]{0:T(1024)S(1)}, f32[1024]{0:T(1024)}, u32[]{:S(2)}) copy-start(f32[1024]{0:T(1024)} %copy-done.48) | copy-start | bytes 12292
  659.8 21.1 %copy-start.55 = (f32[1024]{0:T(1024)S(1)}, f32[1024]{0:T(1024)}, u32[]{:S(2)}) copy-start(f32[1024]{0:T(1024)} %copy-done.54) | copy-start | bytes 12292
  690.5 82.1 %copy-start.26 = (bf16[1024,16]{0,1:T(8,128)(2,1)S(1)}, bf16[1024,16]{0,1:T(8,128)(2,1)}, u32[]{:S(2)}) copy-start(bf16[1024,16]{0,1:T(8,128)(2,1)} %copy-done.25) | copy-start | bytes 98308
  690.5 86.8 %copy-start.38 = (bf16[2,8,768]{2,1,0:T(8,128)(2,1)S(1)}, bf16[2,8,768]{2,1,0:T(8,128)(2,1)}, u32[]{:S(2)}) copy-start(bf16[2,8,768]{2,1,0:T(8,128)(2,1)} %copy-done.35) | copy-start | bytes 73732
  701.2 11.6 %slice-start.3 = ((s8[12582912]{0:T(1024)(128)(4,1)}), s8[4194304]{0:T(1024)(128)(4,1)S(1)}, s32[]{:S(2)}) async-start(s8[12582912]{0:T(1024)(128)(4,1)} %bitcast.331), calls=%async_computation.13 | async-start | bytes 8388608 | tf_op jit(solution)/shard_map/while
  701.2 11.6 %slice-start.4 = ((s8[12582912]{0:T(1024)(128)(4,1)}), s8[4194304]{0:T(1024)(128)(4,1)S(1)}, s32[]{:S(2)}) async-start(s8[12582912]{0:T(1024)(128)(4,1)} %bitcast.331), calls=%async_computation.14 | async-start | bytes 8388608 | tf_op jit(solution)/shard_map/while
  701.2 12.0 %slice-start.5 = ((s8[12582912]{0:T(1024)(128)(4,1)}), s8[4194304]{0:T(1024)(128)(4,1)S(1)}, s32[]{:S(2)}) async-start(s8[12582912]{0:T(1024)(128)(4,1)} %bitcast.331), calls=%async_computation.15 | async-start | bytes 8388608 | tf_op jit(solution)/shard_map/while
  742.1 11.6 %slice-start.3 = ((s8[12582912]{0:T(1024)(128)(4,1)}), s8[4194304]{0:T(1024)(128)(4,1)S(1)}, s32[]{:S(2)}) async-start(s8[12582912]{0:T(1024)(128)(4,1)} %bitcast.331), calls=%async_computation.13 | async-start | bytes 8388608 | tf_op jit(solution)/shard_map/while
  742.2 11.6 %slice-start.4 = ((s8[12582912]{0:T(1024)(128)(4,1)}), s8[4194304]{0:T(1024)(128)(4,1)S(1)}, s32[]{:S(2)}) async-start(s8[12582912]{0:T(1024)(128)(4,1)} %bitcast.331), calls=%async_computation.14 | async-start | bytes 8388608 | tf_op jit(solution)/shard_map/while
  742.2 12.0 %slice-start.5 = ((s8[12582912]{0:T(1024)(128)(4,1)}), s8[4194304]{0:T(1024)(128)(4,1)S(1)}, s32[]{:S(2)}) async-start(s8[12582912]{0:T(1024)(128)(4,1)} %bitcast.331), calls=%async_computation.15 | async-start | bytes 8388608 | tf_op jit(solution)/shard_map/while
  779.2 9.4 %copy-start.34 = (bf16[2,8,768]{2,1,0:T(8,128)(2,1)S(1)}, bf16[2,8,768]{2,1,0:T(8,128)(2,1)}, u32[]{:S(2)}) copy-start(bf16[2,8,768]{2,1,0:T(8,128)(2,1)} %copy-done.31) | copy-start | bytes 73732
  779.2 16.9 %copy-start.9 = (f32[1024,768]{1,0:T(8,128)S(1)}, f32[1024,768]{1,0:T(8,128)}, u32[]{:S(2)}) copy-start(f32[1024,768]{1,0:T(8,128)} %copy-done.8) | copy-start | bytes 9437188
  779.2 16.9 %copy-start.57 = (f32[1024]{0:T(1024)S(1)}, f32[1024]{0:T(1024)}, u32[]{:S(2)}) copy-start(f32[1024]{0:T(1024)} %copy-done.56) | copy-start | bytes 12292
  779.2 128.3 %all-reduce.8.cloned.1.call-start = ((), (), s32[]{:S(2)}) async-start(), calls=%async_computation.8 | async-start | bytes 196608 | tf_op jit(solution)/shard_map/psum | solution.py:309
  796.1 112.9 %copy-start.1 = (bf16[2,80,768]{2,1,0:T(8,128)(2,1)S(1)}, bf16[2,80,768]{2,1,0:T(8,128)(2,1)}, u32[]{:S(2)}) copy-start(bf16[2,80,768]{2,1,0:T(8,128)(2,1)} %param.21) | copy-start | bytes 737284
  (40 other events, 162.1 us)
Sparse Core Ops, SparseCore 0:
  11.5 61.3 all-gather.20
  76.4 52.4 all-gather.22
  131.7 63.7 all-gather.24
  198.3 62.4 all-gather.26
  263.5 57.8 all-gather.28
  324.8 52.4 all-gather.30
  380.2 63.9 all-gather.32
  447.0 62.4 all-gather.34
  779.3 16.7 all-reduce.9
  801.9 105.6 all-reduce.7
